TPU v7x, 256 devices: a whole 4x4x8 slice. The times are simulated.
256 devices in a mesh: dp: 128 (over y, z, x), rep: 2 (over core).
Axes of the slice: x: 4, y: 4, z: 8, core: 2. Of those that a mesh axis runs over, the one named last changes fastest.
Arguments:
- embeddings: float32 [131072, 1024], P(('dp', 'rep')), may hold values from -6 to 6
- cluster_ids: int32 [131072, 1], P(('dp', 'rep')), may hold values from 0 to 255; in each aligned block of 512 rows (0 to 511, 512 to 1023, ...) at most 4 rows name the same one
- boundary_slots: int32 [256, 2, 256], P(('dp', 'rep')), may hold values from 0 to 1023
Outputs:
- member_max: float32 [256, 1024], P(('dp', 'rep'))
- centrality: float32 [256, 1024], P(('dp', 'rep'))
Inputs may be any that keep to these rules, and one draw needn't show every extreme that they name: `cluster_ids`: among the rows of one device, at most 4 name the same cluster, a bound that some block reaches of them; every cluster is named by some row.
All inputs are finite; a program needn't handle non-finite values.
Results may differ from a plain program's by a relative error of at most 0.0024.
Values may be sent and summed in bfloat16 or wider, within the bound.
A program may use at most 64 MiB of HBM per device.

v0:
```python
import jax
import jax.numpy as jnp
from jax import lax
from jax.sharding import PartitionSpec as P

SLOTS = 1024
eps = 1e-06


def from_behind(array, axis, by):
    peers = lax.axis_size(axis)
    pairs = [(i, i + by) for i in range(peers) if 0 <= i + by < peers]
    return lax.ppermute(array, axis, pairs)


def per_device(embeddings, cluster_ids, boundary_slots):
    n_chips = lax.axis_size("dp")
    n_cores = lax.axis_size("rep")
    owners = n_chips * n_cores
    width = embeddings.shape[1]
    slots = SLOTS
    capacity = slots // owners
    bound = boundary_slots.shape[2]
    me = lax.axis_index(("dp", "rep"))
    labels = cluster_ids[:, 0]
    member_of = labels[:, None] == jnp.arange(owners, dtype=jnp.int32)[None, :]
    running = jnp.cumsum(member_of.astype(jnp.int32), axis=0)
    ranks = jnp.sum(jnp.where(member_of, running, 0), axis=1) - 1
    targets = labels * capacity + ranks
    unit_full = embeddings * lax.rsqrt(
        jnp.sum(embeddings * embeddings, axis=1, keepdims=True) + eps
    )
    unit_half = unit_full.astype(jnp.bfloat16)
    outgoing = jnp.zeros((slots, width), jnp.bfloat16).at[targets].set(unit_half)
    member_half = member_of.astype(jnp.bfloat16)
    shaped = outgoing.reshape(n_chips, n_cores, capacity, width)
    arrived = lax.all_to_all(
        lax.all_to_all(shaped, "dp", split_axis=0, concat_axis=0, tiled=True),
        "rep",
        split_axis=1,
        concat_axis=1,
        tiled=True,
    )
    members = arrived.reshape(slots, width)
    partial_sums = lax.dot_general(
        member_half, unit_half, (((0,), (0,)), ((), ())), preferred_element_type=jnp.float32
    )
    total = lax.psum(partial_sums, ("dp", "rep"))
    own_sum = lax.dynamic_slice_in_dim(total, me, 1, 0)
    direction = own_sum[0] * lax.rsqrt(jnp.sum(own_sum * own_sum) + eps)
    lengths = jnp.einsum("se,se->s", members, members, preferred_element_type=jnp.float32)
    filled = lengths > 0.5
    filled_int = filled.astype(jnp.int32)
    count = jnp.sum(filled_int)
    order = jnp.argsort(1 - filled_int, stable=True)
    picks = boundary_slots[0] % count
    positions = order[picks.reshape(-1)]
    outward = members[positions]
    lower = from_behind(outward[bound:], ("dp", "rep"), 1)
    upper = from_behind(outward[:bound], ("dp", "rep"), -1)
    candidates = jnp.concatenate([members, lower, upper], axis=0)
    cand_ok = jnp.concatenate(
        [filled, jnp.full((bound,), me > 0), jnp.full((bound,), me < owners - 1)]
    )
    column = jnp.arange(slots + 2 * bound, dtype=jnp.int32)
    block = min(512, slots)

    def one_block(start):
        block_rows = lax.dynamic_slice_in_dim(members, start, block, 0)
        scores = lax.dot_general(
            block_rows, candidates, (((1,), (1,)), ((), ())), preferred_element_type=jnp.float32
        )
        row_pos = start + jnp.arange(block, dtype=jnp.int32)
        keep = cand_ok[None, :] & (column[None, :] != row_pos[:, None])
        return jnp.max(jnp.where(keep, scores, -1.0), axis=1)

    starts = jnp.arange(slots // block, dtype=jnp.int32) * block
    best = lax.map(one_block, starts).reshape(slots)
    member_max = jnp.where(filled, best, 0.0)
    central = jnp.dot(
        members, direction, precision=lax.Precision.HIGHEST, preferred_element_type=jnp.float32
    )
    centrality = jnp.where(filled, central, 0.0)
    return (member_max[None, :], centrality[None, :])


def solution(mesh):
    placed = (P(("dp", "rep"), None), P(("dp", "rep"), None), P(("dp", "rep"), None, None))
    return jax.shard_map(
        per_device,
        mesh=mesh,
        in_specs=placed,
        out_specs=(P(("dp", "rep"), None), P(("dp", "rep"), None)),
        check_vma=False,
    )
```

profile of v0, /device:TPU:8, one launch (start us, length us, event | category | flops | bytes accessed | tf_op | source)
XLA Modules:
  0.0 374.8 jit_solution(14825172263603566123)
XLA Ops:
  7.2 0.0 copy-start.1
  7.2 1.8 multiply_reduce_fusion
  9.0 0.0 copy-start
  9.0 0.0 copy-done.1
  9.0 0.1 copy.12
  9.1 0.2 fusion.10
  9.4 0.1 copy.13
  9.5 0.2 fusion.9
  9.8 0.8 copy-done
  10.6 4.2 %scatter_custom_fusion = bf16[1024,1024]{1,0:T(8,128)(2,1)} fusion(s32[512]{0:T(512)S(1)} %bitcast.58, bf16[]{:T(256)} %constant.27.clone.1, f32[512,1024]{1,0:T(8,128)S(1)} %copy-done, f32[512]{0:T(512)S(1)} %add_rsqrt_fusion), kind=kCustom, calls=%fused_computation.16 | custom fusion | flops 1048576 | bytes 4196354 | tf_op jit(solution)/shard_map/scatter | solution.py:34
  14.7 4.1 %reshape.106 = bf16[128,2,4,1024]{3,2,1,0:T(4,128)(2,1)} reshape(bf16[1024,1024]{1,0:T(8,128)(2,1)} %scatter_custom_fusion) | data formatting | bytes 4194304 | tf_op jit(solution)/shard_map/reshape | solution.py:36
  18.8 15.9 %all-to-all-start = ((bf16[128,2,4,1024]{3,2,1,0:T(4,128)(2,1)}), bf16[128,2,4,1024]{3,2,1,0:T(4,128)(2,1)}, u32[]{:S(2)}, u32[]{:S(2)}) async-start(bf16[128,2,4,1024]{3,2,1,0:T(4,128)(2,1)} %reshape.106), calls=%async_computation | async-start | bytes 4194304 | tf_op jit(solution)/shard_map/all_to_all | solution.py:38
  34.8 0.0 all-reduce.2.cloned.1.call-start
  34.8 1.7 fusion.12
  36.5 0.0 all-reduce.2.cloned.1.call-update
  36.5 268.0 %all-reduce.2.cloned.1.call-done = f32[256,1024]{1,0:T(8,128)} async-done(((f32[256,1024]{1,0:T(8,128)}), f32[256,1024]{1,0:T(8,128)}) %all-reduce.2.cloned.1.call-update) | async-done | bytes 1048592 | tf_op jit(solution)/shard_map/psum | solution.py:48
  304.5 1.4 multiply_reduce_fusion.1
  306.6 0.0 all-to-all-done
  306.6 2.3 copy.14
  308.9 5.4 %all_to_all.10 = bf16[128,2,4,1024]{3,2,0,1:T(4,128)(2,1)S(1)} all-to-all(bf16[128,2,4,1024]{3,2,0,1:T(4,128)(2,1)S(1)} %copy.14), channel_id=1, replica_groups=mesh['dp'=128,'rep'=2] {'rep'}, dimensions={1} | all-to-all | bytes 4194304 | tf_op jit(solution)/shard_map/all_to_all | solution.py:37
  314.3 2.6 copy.15
  317.0 2.5 reshape.107
  319.5 0.0 copy-start.2
  319.5 0.5 fusion.6
  320.0 2.5 fusion.15
  322.5 0.6 broadcast_select_fusion
  323.1 0.6 convert_reduce_fusion
  325.0 0.0 copy-done.2
  325.0 0.1 remainder_bitcast_fusion
  325.2 4.4 %sort.17 = (s32[1024]{0:T(1024)}, s32[1024]{0:T(1024)S(1)}) sort(s32[1024]{0:T(1024)S(1)} %get-tuple-element.73, s32[1024]{0:T(1024)S(1)} %iota.25), dimensions={0}, to_apply=%region_5.6 | sort | flops 10240 | bytes 16384 | tf_op jit(solution)/shard_map/jit(argsort)/sort | solution.py:55
  329.6 2.3 gather_fusion
  331.9 2.1 gather_fusion.1
  334.0 1.1 fusion.21
  335.0 2.0 collective-permute-start
  337.1 7.7 %collective-permute-start.1 = (bf16[256,1024]{1,0:T(8,128)(2,1)}, bf16[256,1024]{1,0:T(8,128)(2,1)S(1)}, u32[]{:S(2)}, u32[]{:S(2)}) collective-permute-start(bf16[256,1024]{1,0:T(8,128)(2,1)} %get-tuple-element.71), channel_id=1, source_target_pairs={{1,0},{2,1},{3,2},{4,3},{5,4},{6,5},{7,6},{8,7},{9,8},{10,9},{11,1... | collective-permute-start | bytes 1572872 | tf_op jit(solution)/shard_map/ppermute | solution.py:13
  344.9 5.1 %collective-permute-done = bf16[256,1024]{1,0:T(8,128)(2,1)S(1)} collective-permute-done((bf16[256,1024]{1,0:T(8,128)(2,1)}, bf16[256,1024]{1,0:T(8,128)(2,1)S(1)}, u32[]{:S(2)}, u32[]{:S(2)}) %collective-permute-start) | collective-permute-done | bytes 524320 | tf_op jit(solution)/shard_map/ppermute | solution.py:13
  349.9 1.9 collective-permute-done.1
  351.8 1.9 pad_maximum_fusion
  353.7 13.6 %while.11 = (s32[]{:T(128)}, f32[2,512]{1,0:T(2,128)S(1)}, pred[1536]{0:T(1024)(128)(4,1)S(1)}, s32[2]{0:T(128)S(1)}, bf16[1024,1024]{1,0:T(8,128)(2,1)S(1)}, /*...) while((s32[]{:T(128)}, f32[2,512]{1,0:T(2,128)S(1)}, ...), condition=%wide.region_9.10_spmd.clone, body=%wide.region_7.9_spmd.clone.sunk | while | flops 1613758464 | bytes 4206743 | solution.py:78
  353.7 0.5 dynamic_slice.23
  355.9 0.5 iota_add_fusion.2
  356.4 4.0 %fusion.29 = f32[512]{0:T(512)S(1)} fusion(bf16[1536,1024]{1,0:T(8,128)(2,1)} %get-tuple-element.134, s32[512]{0:T(512)S(1)} %iota_add_fusion.2, pred[1536]{0:T(1024)(128)(4,1)S(1)} %get-tuple-element.131, bf16[1024,1024]{1,0:T(8,128)(2,1)S(1)} %get-tuple-element.133, s32[]{:T(128)S(6)} %select_n.90), kind=kOutput, calls=%fused_computation.7.clone.1 | convolution fusion | flops 1613757952 | bytes 4200452 | tf_op jit(solution)/shard_map/while/body/eval_jaxpr/dot_general | solution.py:70
  360.5 0.6 dynamic_slice.23
  362.7 0.5 iota_add_fusion.2
  363.2 4.0 %fusion.29 = f32[512]{0:T(512)S(1)} fusion(bf16[1536,1024]{1,0:T(8,128)(2,1)} %get-tuple-element.134, s32[512]{0:T(512)S(1)} %iota_add_fusion.2, pred[1536]{0:T(1024)(128)(4,1)S(1)} %get-tuple-element.131, bf16[1024,1024]{1,0:T(8,128)(2,1)S(1)} %get-tuple-element.133, s32[]{:T(128)S(6)} %select_n.90), kind=kOutput, calls=%fused_computation.7.clone.1 | convolution fusion | flops 1613757952 | bytes 4200452 | tf_op jit(solution)/shard_map/while/body/eval_jaxpr/dot_general | solution.py:70
  367.3 0.6 broadcast_select_fusion.1
  (22 shorter events, 0.2 us)
Async XLA Ops:
  7.2 1.8 copy-start.1
  9.0 1.6 copy-start
  18.8 287.7 %all-to-all-start = ((bf16[128,2,4,1024]{3,2,1,0:T(4,128)(2,1)}), bf16[128,2,4,1024]{3,2,1,0:T(4,128)(2,1)}, u32[]{:S(2)}, u32[]{:S(2)}) async-start(bf16[128,2,4,1024]{3,2,1,0:T(4,128)(2,1)} %reshape.106), calls=%async_computation | async-start | bytes 4194304 | tf_op jit(solution)/shard_map/all_to_all | solution.py:38
  34.8 269.8 %all-reduce.2.cloned.1.call-start = ((), (), s32[]{:S(2)}) async-start(), calls=%async_computation.2 | async-start | bytes 2097152 | tf_op jit(solution)/shard_map/psum | solution.py:48
  319.5 5.5 %copy-start.2 = (s32[1,2,256]{2,1,0:T(2,128)S(1)}, s32[1,2,256]{2,1,0:T(2,128)}, u32[]{:S(2)}) copy-start(s32[1,2,256]{2,1,0:T(2,128)} %param.7) | copy-start | bytes 6148
  335.0 14.9 %collective-permute-start = (bf16[256,1024]{1,0:T(8,128)(2,1)}, bf16[256,1024]{1,0:T(8,128)(2,1)S(1)}, u32[]{:S(2)}, u32[]{:S(2)}) collective-permute-start(bf16[256,1024]{1,0:T(8,128)(2,1)} %get-tuple-element.70), channel_id=1, source_target_pairs={{0,1},{1,2},{2,3},{3,4},{4,5},{5,6},{6,7},{7,8},{8,9},{9,10},{10,1... | collective-permute-start | bytes 1572872 | tf_op jit(solution)/shard_map/ppermute | solution.py:13
  337.1 14.7 %collective-permute-start.1 = (bf16[256,1024]{1,0:T(8,128)(2,1)}, bf16[256,1024]{1,0:T(8,128)(2,1)S(1)}, u32[]{:S(2)}, u32[]{:S(2)}) collective-permute-start(bf16[256,1024]{1,0:T(8,128)(2,1)} %get-tuple-element.71), channel_id=1, source_target_pairs={{1,0},{2,1},{3,2},{4,3},{5,4},{6,5},{7,6},{8,7},{9,8},{10,9},{11,1... | collective-permute-start | bytes 1572872 | tf_op jit(solution)/shard_map/ppermute | solution.py:13
Sparse Core Ops, SparseCore 0:
  41.0 263.4 all-reduce.1
where the time goes:
time: 376 us; the launch traced here: 375 us
  waiting for transfers between devices  275 us (73%)
  starting transfers between devices  25.7 us (7%)
  local copies, waits for them, and re-layouts  19.2 us (5%)
  other arithmetic  17.7 us (5%)
  between operations  16.3 us (4%)
  matrix products  12.1 us (3%)
  blocking collectives  5.42 us (1%)
    psum x1, waiting for transfers between devices, per_device(): total = lax.psum(partial_sums, ('dp', 'rep'))  268 us
    all_to_all x1, starting transfers between devices, per_device(): lax.all_to_all(shaped, 'dp', split_axis=0, concat_axis=0, tiled=True)  15.9 us
    ppermute x2, starting transfers between devices, from_behind(): return lax.ppermute(array, axis, pairs)  9.77 us
    dot_general x2, matrix products, one_block(): lax.dot_general(block_rows, candidates, (((1,), (1,)), ((), ())), preferr...  8.01 us
  transfers between devices with their start and end apart: 4, of which 3 were waited for; matrix products, arithmetic and copies ran while one was open for 1% of the time, Pallas kernels for 0%

commit v1 on v0

--- a/solution.py
+++ b/solution.py
@@ -34,13 +34,11 @@
     outgoing = jnp.zeros((slots, width), jnp.bfloat16).at[targets].set(unit_half)
     member_half = member_of.astype(jnp.bfloat16)
     shaped = outgoing.reshape(n_chips, n_cores, capacity, width)
-    arrived = lax.all_to_all(
-        lax.all_to_all(shaped, "dp", split_axis=0, concat_axis=0, tiled=True),
-        "rep",
-        split_axis=1,
-        concat_axis=1,
-        tiled=True,
-    )
+    own = lax.all_to_all(shaped, "dp", split_axis=0, concat_axis=0, tiled=True)
+    devices = lax.axis_size("rep")
+    shards = jnp.stack(jnp.split(own, devices, axis=1), axis=0)
+    shards = lax.all_to_all(shards, "rep", split_axis=0, concat_axis=0)
+    arrived = jnp.concatenate(shards, axis=1)
     members = arrived.reshape(slots, width)
     partial_sums = lax.dot_general(
         member_half, unit_half, (((0,), (0,)), ((), ())), preferred_element_type=jnp.float32

time: 376 us -> 377 us (level)
    all_to_all x2 -> x0, local copies, waits for them, and re-layouts: 4.94 us -> none  [the longest x1 2.63 us: per_device(): lax.all_to_all(lax.all_to_all(shaped, 'dp', split_axis=0, concat_axis=0,...]
    another operation x3 -> x5, local copies, waits for them, and re-layouts: 0.11 us -> 4.91 us  [the longest x1 2.54 us: per_device(): members = arrived.reshape(slots, width)]
where the time goes in v1:
time: 377 us; the launch traced here: 376 us
  waiting for transfers between devices  275 us (73%)
  starting transfers between devices  25.7 us (7%)
  local copies, waits for them, and re-layouts  19.2 us (5%)
  other arithmetic  19.2 us (5%)
  between operations  16.3 us (4%)
  matrix products  12.1 us (3%)
  blocking collectives  5.42 us (1%)
    psum x1, waiting for transfers between devices, per_device(): total = lax.psum(partial_sums, ('dp', 'rep'))  268 us
    all_to_all x1, starting transfers between devices, per_device(): own = lax.all_to_all(shaped, 'dp', split_axis=0, concat_axis=0, tiled=True)  15.9 us
    ppermute x2, starting transfers between devices, from_behind(): return lax.ppermute(array, axis, pairs)  9.77 us
    dot_general x2, matrix products, one_block(): lax.dot_general(block_rows, candidates, (((1,), (1,)), ((), ())), preferr...  8.01 us
  transfers between devices with their start and end apart: 4, of which 3 were waited for; matrix products, arithmetic and copies ran while one was open for 1% of the time, Pallas kernels for 0%

profile of v1, /device:TPU:8, one launch (start us, length us, event | category | flops | bytes accessed | tf_op | source)
XLA Modules:
  0.0 376.2 jit_solution(17758107287226644432)
XLA Ops:
  7.2 0.0 copy-start.1
  7.2 1.8 multiply_reduce_fusion
  9.0 0.0 copy-start
  9.0 0.0 copy-done.1
  9.0 0.1 copy.7
  9.1 0.2 fusion.10
  9.4 0.1 copy.8
  9.5 0.2 fusion.9
  9.8 0.8 copy-done
  10.6 4.2 %scatter_custom_fusion = bf16[1024,1024]{1,0:T(8,128)(2,1)} fusion(s32[512]{0:T(512)S(1)} %bitcast.68, bf16[]{:T(256)} %constant.27.clone.1, f32[512,1024]{1,0:T(8,128)S(1)} %copy-done, f32[512]{0:T(512)S(1)} %add_rsqrt_fusion), kind=kCustom, calls=%fused_computation.19 | custom fusion | flops 1048576 | bytes 4196354 | tf_op jit(solution)/shard_map/scatter | solution.py:34
  14.7 4.1 %reshape.106 = bf16[128,2,4,1024]{3,2,1,0:T(4,128)(2,1)} reshape(bf16[1024,1024]{1,0:T(8,128)(2,1)} %scatter_custom_fusion) | data formatting | bytes 4194304 | tf_op jit(solution)/shard_map/reshape | solution.py:36
  18.8 15.9 %all-to-all-start = ((bf16[128,2,4,1024]{3,2,1,0:T(4,128)(2,1)}), bf16[128,2,4,1024]{3,2,1,0:T(4,128)(2,1)}, u32[]{:S(2)}, u32[]{:S(2)}) async-start(bf16[128,2,4,1024]{3,2,1,0:T(4,128)(2,1)} %reshape.106), calls=%async_computation | async-start | bytes 4194304 | tf_op jit(solution)/shard_map/all_to_all | solution.py:37
  34.8 0.0 all-reduce.2.cloned.1.call-start
  34.8 1.7 fusion.12
  36.5 0.0 all-reduce.2.cloned.1.call-update
  36.5 268.0 %all-reduce.2.cloned.1.call-done = f32[256,1024]{1,0:T(8,128)} async-done(((f32[256,1024]{1,0:T(8,128)}), f32[256,1024]{1,0:T(8,128)}) %all-reduce.2.cloned.1.call-update) | async-done | bytes 1048592 | tf_op jit(solution)/shard_map/psum | solution.py:46
  304.5 1.4 multiply_reduce_fusion.1
  306.6 0.0 all-to-all-done
  306.6 2.3 slice_bitcast_fusion.1
  308.9 1.5 pad_maximum_fusion.1
  310.4 5.4 %all_to_all.10 = bf16[2,128,1,4,1024]{4,3,1,2,0:T(4,128)(2,1)S(1)} all-to-all(bf16[2,128,1,4,1024]{4,3,1,2,0:T(4,128)(2,1)S(1)} %pad_maximum_fusion.1), channel_id=1, replica_groups=mesh['dp'=128,'rep'=2] {'rep'}, dimensions={0} | all-to-all | bytes 4194304 | tf_op jit(solution)/shard_map/all_to_all | solution.py:40
  315.8 2.6 copy.10
  318.4 2.5 reshape_reshape.3
  320.9 0.0 copy-start.2
  321.0 0.5 fusion.6
  321.4 2.5 fusion.15
  323.9 0.6 broadcast_select_fusion
  324.5 0.6 convert_reduce_fusion
  326.5 0.0 copy-done.2
  326.5 0.1 remainder_bitcast_fusion
  326.7 4.4 %sort.17 = (s32[1024]{0:T(1024)}, s32[1024]{0:T(1024)S(1)}) sort(s32[1024]{0:T(1024)S(1)} %get-tuple-element.75, s32[1024]{0:T(1024)S(1)} %iota.25), dimensions={0}, to_apply=%region_5.6 | sort | flops 10240 | bytes 16384 | tf_op jit(solution)/shard_map/jit(argsort)/sort | solution.py:53
  331.0 2.3 gather_fusion
  333.3 2.1 gather_fusion.1
  335.4 1.1 fusion.21
  336.5 2.1 collective-permute-start
  338.6 7.7 %collective-permute-start.1 = (bf16[256,1024]{1,0:T(8,128)(2,1)}, bf16[256,1024]{1,0:T(8,128)(2,1)S(1)}, u32[]{:S(2)}, u32[]{:S(2)}) collective-permute-start(bf16[256,1024]{1,0:T(8,128)(2,1)} %get-tuple-element.73), channel_id=1, source_target_pairs={{1,0},{2,1},{3,2},{4,3},{5,4},{6,5},{7,6},{8,7},{9,8},{10,9},{11,1... | collective-permute-start | bytes 1572872 | tf_op jit(solution)/shard_map/ppermute | solution.py:13
  346.3 5.1 %collective-permute-done = bf16[256,1024]{1,0:T(8,128)(2,1)S(1)} collective-permute-done((bf16[256,1024]{1,0:T(8,128)(2,1)}, bf16[256,1024]{1,0:T(8,128)(2,1)S(1)}, u32[]{:S(2)}, u32[]{:S(2)}) %collective-permute-start) | collective-permute-done | bytes 524320 | tf_op jit(solution)/shard_map/ppermute | solution.py:13
  351.4 1.9 collective-permute-done.1
  353.2 1.9 pad_maximum_fusion
  355.1 13.6 %while.11 = (s32[]{:T(128)}, f32[2,512]{1,0:T(2,128)S(1)}, pred[1536]{0:T(1024)(128)(4,1)S(1)}, s32[2]{0:T(128)S(1)}, bf16[1024,1024]{1,0:T(8,128)(2,1)S(1)}, /*...) while((s32[]{:T(128)}, f32[2,512]{1,0:T(2,128)S(1)}, ...), condition=%wide.region_9.10_spmd.clone, body=%wide.region_7.9_spmd.clone.sunk | while | flops 1613758464 | bytes 4206743 | solution.py:76
  355.1 0.5 dynamic_slice.23
  357.3 0.5 iota_add_fusion.2
  357.9 4.0 %fusion.29 = f32[512]{0:T(512)S(1)} fusion(bf16[1536,1024]{1,0:T(8,128)(2,1)} %get-tuple-element.136, s32[512]{0:T(512)S(1)} %iota_add_fusion.2, pred[1536]{0:T(1024)(128)(4,1)S(1)} %get-tuple-element.133, bf16[1024,1024]{1,0:T(8,128)(2,1)S(1)} %get-tuple-element.135, s32[]{:T(128)S(6)} %select_n.90), kind=kOutput, calls=%fused_computation.7.clone.1 | convolution fusion | flops 1613757952 | bytes 4200452 | tf_op jit(solution)/shard_map/while/body/eval_jaxpr/dot_general | solution.py:68
  361.9 0.6 dynamic_slice.23
  364.1 0.5 iota_add_fusion.2
  364.7 4.0 %fusion.29 = f32[512]{0:T(512)S(1)} fusion(bf16[1536,1024]{1,0:T(8,128)(2,1)} %get-tuple-element.136, s32[512]{0:T(512)S(1)} %iota_add_fusion.2, pred[1536]{0:T(1024)(128)(4,1)S(1)} %get-tuple-element.133, bf16[1024,1024]{1,0:T(8,128)(2,1)S(1)} %get-tuple-element.135, s32[]{:T(128)S(6)} %select_n.90), kind=kOutput, calls=%fused_computation.7.clone.1 | convolution fusion | flops 1613757952 | bytes 4200452 | tf_op jit(solution)/shard_map/while/body/eval_jaxpr/dot_general | solution.py:68
  368.8 0.6 broadcast_select_fusion.1
  (22 shorter events, 0.2 us)
Async XLA Ops:
  7.2 1.8 copy-start.1
  9.0 1.6 copy-start
  18.8 287.7 %all-to-all-start = ((bf16[128,2,4,1024]{3,2,1,0:T(4,128)(2,1)}), bf16[128,2,4,1024]{3,2,1,0:T(4,128)(2,1)}, u32[]{:S(2)}, u32[]{:S(2)}) async-start(bf16[128,2,4,1024]{3,2,1,0:T(4,128)(2,1)} %reshape.106), calls=%async_computation | async-start | bytes 4194304 | tf_op jit(solution)/shard_map/all_to_all | solution.py:37
  34.8 269.8 %all-reduce.2.cloned.1.call-start = ((), (), s32[]{:S(2)}) async-start(), calls=%async_computation.2 | async-start | bytes 2097152 | tf_op jit(solution)/shard_map/psum | solution.py:46
  320.9 5.5 %copy-start.2 = (s32[1,2,256]{2,1,0:T(2,128)S(1)}, s32[1,2,256]{2,1,0:T(2,128)}, u32[]{:S(2)}) copy-start(s32[1,2,256]{2,1,0:T(2,128)} %param.7) | copy-start | bytes 6148
  336.5 14.9 %collective-permute-start = (bf16[256,1024]{1,0:T(8,128)(2,1)}, bf16[256,1024]{1,0:T(8,128)(2,1)S(1)}, u32[]{:S(2)}, u32[]{:S(2)}) collective-permute-start(bf16[256,1024]{1,0:T(8,128)(2,1)} %get-tuple-element.72), channel_id=1, source_target_pairs={{0,1},{1,2},{2,3},{3,4},{4,5},{5,6},{6,7},{7,8},{8,9},{9,10},{10,1... | collective-permute-start | bytes 1572872 | tf_op jit(solution)/shard_map/ppermute | solution.py:13
  338.6 14.7 %collective-permute-start.1 = (bf16[256,1024]{1,0:T(8,128)(2,1)}, bf16[256,1024]{1,0:T(8,128)(2,1)S(1)}, u32[]{:S(2)}, u32[]{:S(2)}) collective-permute-start(bf16[256,1024]{1,0:T(8,128)(2,1)} %get-tuple-element.73), channel_id=1, source_target_pairs={{1,0},{2,1},{3,2},{4,3},{5,4},{6,5},{7,6},{8,7},{9,8},{10,9},{11,1... | collective-permute-start | bytes 1572872 | tf_op jit(solution)/shard_map/ppermute | solution.py:13
Sparse Core Ops, SparseCore 0:
  41.0 263.4 all-reduce.1
